TPU v7x, 32 devices: a whole 2x2x4 slice. The times are simulated.
32 devices in a mesh: wide: 8 (over y, x, core), narrow: 4 (over z).
Axes of the slice: x: 2, y: 2, z: 4, core: 2. Of those that a mesh axis runs over, the one named last changes fastest.
Arguments:
- hidden: bfloat16 [1024, 4096], P('wide', 'narrow'), may hold values from -6 to 6
- head_weight: bfloat16 [32768, 4096], P('wide', 'narrow'), may hold values from -0.25 to 0.25
- lse: float32 [1024], replicated, may hold values from 12 to 14
- targets: int32 [1024], replicated, may hold values from 0 to 32767
- loss_weight: float32 [1024], replicated, may hold values from 16 to 48
- block_tiles: int32 [8, 8, 4], P(None, 'wide'), may hold values from 0 to 31, as said below
- block_counts: int32 [8, 8], P(None, 'wide'), may hold values from 0 to 4, as said below
- gate_pre: bfloat16 [1024, 7168], P('wide', 'narrow'), may hold values from -6 to 6
- up_pre: bfloat16 [1024, 7168], P('wide', 'narrow'), may hold values from -6 to 6
- down_weight: bfloat16 [7168, 4096], P('narrow'), may hold values from -0.0625 to 0.0625
Outputs:
- head_grad: bfloat16 [1024, 4096], P('wide', 'narrow')
- gate_grad: bfloat16 [1024, 7168], P('wide', 'narrow')
- up_grad: bfloat16 [1024, 7168], P('wide', 'narrow')
Inputs may be any that keep to these rules, and one draw needn't show every extreme that they name: The first block_counts[b, s] entries of block_tiles[b, s] are distinct; the other entries are ignored. `block_counts`: some row block has 4 active tiles in some shard; one shard has exactly 16 active tiles over all row blocks, and no shard has more.
All inputs are finite; a program needn't handle non-finite values.
Results may differ from a plain program's by a relative error of at most 0.0035.
The roundings to bfloat16 on the way count: a program that leaves them out, or rounds other values in their place, can miss the bound.
Values may be sent and summed in bfloat16 or wider, within the bound.
No kernel may reach another device: no remote copies, remote signals or barrier semaphores. Data moves between devices by JAX's collectives and lax.ppermute only.
A program may use at most 128 MiB of HBM per device.

v0:
```python
import jax
import jax.numpy as jnp
from jax import lax
from jax.sharding import PartitionSpec as P

TILE = 128


def slot_table(tiles_here, counts_here, slot_count):
    block_total, per_block = tiles_here.shape
    slot_live = (jnp.arange(per_block, dtype=jnp.int32)[None, :] < counts_here[:, None]).reshape(-1)
    position = jnp.cumsum(slot_live.astype(jnp.int32)) - 1
    select = (position[None, :] == jnp.arange(slot_count, dtype=jnp.int32)[:, None]) & slot_live[
        None, :
    ]
    chosen = select.astype(jnp.int32)
    block_ids = jnp.repeat(jnp.arange(block_total, dtype=jnp.int32), per_block)
    slot_blocks = jnp.sum(chosen * block_ids[None, :], axis=1)
    slot_tiles = jnp.sum(chosen * tiles_here.reshape(-1)[None, :], axis=1)
    return (slot_blocks, slot_tiles, jnp.sum(chosen, axis=1) > 0)


def cell_weights(logits, lse_rows, scale_rows, slot_live):
    scaled = jnp.exp(logits - lse_rows[:, :, None]) * scale_rows[:, :, None]
    return jnp.where(slot_live[:, None, None], scaled, 0.0).astype(jnp.bfloat16)


def on_device(
    hidden,
    head_weight,
    lse,
    targets,
    loss_weight,
    block_tiles,
    block_counts,
    gate_pre,
    up_pre,
    down_weight,
):
    features = hidden.shape[1]
    row_count = hidden.shape[0]
    vocab_here = head_weight.shape[0]
    offset = lax.axis_index("wide") * vocab_here
    gathered = lax.all_gather(hidden, "wide", axis=0, tiled=True)
    blocks = gathered.shape[0] // TILE
    weight_tiles = head_weight.reshape(vocab_here // TILE, TILE, features)
    tiles_here = block_tiles[:, 0, :]
    counts_here = block_counts[:, 0]
    per_block = tiles_here.shape[1]
    lse_blocks = lse.reshape(blocks, TILE)
    scale_blocks = loss_weight.reshape(blocks, TILE)
    slot_count = blocks // 2 * per_block
    slot_blocks, slot_tiles, slot_live = slot_table(tiles_here, counts_here, slot_count)
    picked = jnp.take(weight_tiles, slot_tiles, axis=0)
    row_blocks = jnp.take(gathered.reshape(blocks, TILE, features), slot_blocks, axis=0)
    partial_value = jnp.einsum(
        "srd,scd->src", row_blocks, picked, preferred_element_type=jnp.float32
    )
    slot_lse = jnp.take(lse_blocks, slot_blocks, axis=0)
    slot_scale = jnp.take(scale_blocks, slot_blocks, axis=0)
    logits = lax.psum(partial_value, "narrow")
    cell_probs = cell_weights(logits, slot_lse, slot_scale, slot_live)
    contrib = jnp.einsum("src,scd->srd", cell_probs, picked, preferred_element_type=jnp.float32)
    contrib = contrib.reshape(slot_count, TILE * features)
    block_span = row_count * lax.axis_size("wide") // TILE
    wanted = jnp.arange(block_span, dtype=jnp.int32)
    member = ((slot_blocks[None, :] == wanted[:, None]) & slot_live[None, :]).astype(jnp.float32)
    softmax_part = jnp.dot(
        member, contrib, precision=lax.Precision.HIGHEST, preferred_element_type=jnp.float32
    ).reshape(row_count * lax.axis_size("wide"), features)
    local_ids = targets - offset
    inside = (local_ids >= 0) & (local_ids < vocab_here)
    target_rows = jnp.take(head_weight, jnp.clip(local_ids, 0, vocab_here - 1), axis=0).astype(
        jnp.float32
    )
    factor = jnp.where(inside, loss_weight, 0.0)
    head_grad = lax.psum_scatter(
        softmax_part - factor[:, None] * target_rows, "wide", scatter_dimension=0, tiled=True
    ).astype(jnp.bfloat16)
    unit_grad = lax.dot_general(
        lax.all_gather(head_grad, "narrow", axis=1, tiled=True),
        down_weight,
        (((1,), (1,)), ((), ())),
        preferred_element_type=jnp.float32,
    )
    gate_value = gate_pre.astype(jnp.float32)
    up_value = up_pre.astype(jnp.float32)
    gate_sig = jax.nn.sigmoid(gate_value)
    up_grad = (unit_grad * gate_value * gate_sig).astype(jnp.bfloat16)
    gate_grad = (unit_grad * up_value * gate_sig * (1.0 + gate_value * (1.0 - gate_sig))).astype(
        jnp.bfloat16
    )
    return (head_grad, gate_grad, up_grad)


def solution(mesh):
    in_specs = (
        P("wide", "narrow"),
        P("wide", "narrow"),
        P(),
        P(),
        P(),
        P(None, "wide", None),
        P(None, "wide"),
        P("wide", "narrow"),
        P("wide", "narrow"),
        P("narrow", None),
    )
    out_specs = (P("wide", "narrow"), P("wide", "narrow"), P("wide", "narrow"))
    return jax.shard_map(
        on_device, mesh=mesh, in_specs=in_specs, out_specs=out_specs, check_vma=False
    )
```

profile of v0, /device:TPU:0, one launch (start us, length us, event | category | flops | bytes accessed | tf_op | source)
XLA Modules:
  0.0 223.7 jit_solution(11905009591479860913)
XLA Ops:
  7.2 0.0 copy-start
  7.2 0.0 all-gather.3.cloned.1.call-start
  7.2 0.7 all-gather.3.cloned.1.call-update
  7.9 0.0 all-reduce.2.cloned.1.call-start
  8.0 0.7 iota_compare_fusion.2
  8.7 0.1 reshape.201
  8.8 0.1 lt.82
  8.9 0.1 mul.57
  8.9 0.8 copy.18
  9.7 0.1 mul.60
  9.8 0.1 reduce-window.8
  9.8 0.1 add_reduce_fusion
  10.0 0.2 convert_reduce_fusion
  10.1 0.0 copy-done
  10.1 0.6 gather_fusion.3
  10.7 1.2 gather_fusion.4
  12.0 6.1 %gather_fusion.1 = bf16[16,128,1024]{2,1,0:T(8,128)(2,1)} fusion(bf16[32,128,1024]{2,1,0:T(8,128)(2,1)} %bitcast.21, s32[1024]{0:T(1024)S(1)} %pad_clamp_fusion.1), kind=kCustom, calls=%fused_computation.3 | custom fusion | bytes 8388672 | tf_op jit(solution)/shard_map/jit(_take)/gather | solution.py:54
  18.1 22.3 %all-gather.3.cloned.1.call-done = bf16[1024,1024]{1,0:T(8,128)(2,1)} async-done(((bf16[128,1024]{1,0:T(8,128)(2,1)}), bf16[1024,1024]{1,0:T(8,128)(2,1)}) %all-gather.3.cloned.1.call-update) | async-done | bytes 2097168 | tf_op jit(solution)/shard_map/all_gather | solution.py:44
  40.4 4.4 %gather_fusion = bf16[16,128,1024]{2,1,0:T(8,128)(2,1)} fusion(bf16[8,128,1024]{2,1,0:T(8,128)(2,1)} %bitcast.24, s32[1024]{0:T(1024)S(1)} %pad_clamp_fusion.2), kind=kCustom, calls=%fused_computation.2 | custom fusion | bytes 8388672 | tf_op jit(solution)/shard_map/jit(_take)/gather | solution.py:55
  44.8 0.0 copy-start.3
  44.8 6.0 %fusion = f32[16,128,128]{2,1,0:T(8,128)} fusion(bf16[16,128,1024]{2,1,0:T(8,128)(2,1)} %gather_fusion, pred[16]{0:T(512)(128)(4,1)S(1)} %get-tuple-element.14, bf16[16,128,1024]{2,1,0:T(8,128)(2,1)} %gather_fusion.1, pred[16]{0:T(512)(128)(4,1)S(1)} %get-tuple-element.13), kind=kOutput, calls=%fused_computation.6 | convolution fusion | flops 541065216 | bytes 9437216 | tf_op jit(solution)/shard_map/srd,scd->src/dot_general | solution.py:56
  50.8 0.0 all-reduce.2.cloned.1.call-update
  50.8 0.2 reduce-scatter.2.cloned.1.call-start
  51.0 0.0 copy-done.3
  51.1 0.0 copy-start.2
  51.1 9.4 %gather_fusion.2 = bf16[1024,1024]{1,0:T(8,128)(2,1)S(1)} fusion(bf16[4096,1024]{1,0:T(8,128)(2,1)} %param.13, s32[1024]{0:T(1024)S(1)} %fusion.21), kind=kCustom, calls=%fused_computation.4 | custom fusion | bytes 4198400 | tf_op jit(solution)/shard_map/jit(_take)/gather | solution.py:73
  60.6 0.0 copy-done.2
  60.6 0.1 broadcast_select_fusion.4
  60.7 42.2 %all-reduce.2.cloned.1.call-done = f32[16,128,128]{2,1,0:T(8,128)} async-done(((f32[16,128,128]{2,1,0:T(8,128)}), f32[16,128,128]{2,1,0:T(8,128)}) %all-reduce.2.cloned.1.call-update) | async-done | bytes 1048592 | tf_op jit(solution)/shard_map/psum | solution.py:61
  102.9 3.8 %fusion.4 = f32[16,128,1024]{2,1,0:T(8,128)S(1)} fusion(bf16[16,128,1024]{2,1,0:T(8,128)(2,1)} %gather_fusion.1, pred[16]{0:T(512)(128)(4,1)S(1)} %get-tuple-element.13, f32[16,128,128]{2,1,0:T(8,128)} %all-reduce.2.cloned.1.call-done, f32[16,128]{1,0:T(8,128)S(1)} %get-tuple-element.10, f32[16,128]{1,0:T(8,128)S(1)} %get-tuple-element.9, ...), kind=kOutput, calls=%fused_computation.11 | convolution fusion | flops 540016640 | bytes 13647904 | tf_op jit(solution)/shard_map/src,scd->srd/dot_general | solution.py:63
  106.7 4.9 %copy.19 = f32[2,8,128,1024]{3,1,2,0:T(8,128)S(1)} copy(f32[2,8,128,1024]{3,2,1,0:T(8,128)S(1)} %bitcast.22) | data formatting | bytes 16777216
  111.6 4.4 %fusion.19 = f32[8,131072]{1,0:T(8,128)} fusion(f32[16,131072]{1,0:T(8,128)S(1)} %bitcast.23, s32[16]{0:T(128)S(1)} %get-tuple-element.6, pred[16]{0:T(512)(128)(4,1)S(1)} %broadcast_compare_fusion), kind=kOutput, calls=%fused_computation.43 | convolution fusion | flops 201326848 | bytes 12582992 | tf_op jit(solution)/shard_map/dot_general | solution.py:68
  116.0 4.9 %reshape.152 = f32[1024,1024]{1,0:T(8,128)} reshape(f32[8,131072]{1,0:T(8,128)} %fusion.19) | data formatting | bytes 8388608 | tf_op jit(solution)/shard_map/reshape | solution.py:70
  120.9 4.1 %multiply_subtract_fusion = f32[1024,1024]{1,0:T(8,128)} fusion(f32[1024,1024]{1,0:T(8,128)} %reshape.152, bf16[1024,1024]{1,0:T(8,128)(2,1)S(1)} %gather_fusion.2, f32[1024]{0:T(1024)S(1)} %and_select_fusion, pred[1024]{0:T(1024)(128)(4,1)S(1)} %compare_and_fusion), kind=kLoop, calls=%fused_computation.5 | loop fusion | flops 4194304 | bytes 10490880 | tf_op jit(solution)/shard_map/sub | solution.py:78
  125.0 0.0 copy-start.4
  125.0 0.0 copy-start.5
  125.0 0.0 reduce-scatter.2.cloned.1.call-update
  125.0 0.3 all-gather.5.cloned.1.call-start
  125.3 50.3 %reduce-scatter.2.cloned.1.call-done = f32[128,1024]{1,0:T(8,128)} async-done(((f32[1024,1024]{1,0:T(8,128)}), f32[128,1024]{1,0:T(8,128)}) %reduce-scatter.2.cloned.1.call-update) | async-done | bytes 524304 | tf_op jit(solution)/shard_map/reduce_scatter | solution.py:77
  175.6 1.8 convert_element_type.45
  177.3 0.0 all-gather.5.cloned.1.call-update
  177.4 28.2 %all-gather.5.cloned.1.call-done = bf16[128,4096]{1,0:T(8,128)(2,1)} async-done(((bf16[128,1024]{1,0:T(8,128)(2,1)}), bf16[128,4096]{1,0:T(8,128)(2,1)}) %all-gather.5.cloned.1.call-update) | async-done | bytes 1048592 | tf_op jit(solution)/shard_map/all_gather | solution.py:81
  205.6 0.0 copy-done.4
  205.6 0.0 copy-done.5
  205.6 0.0 copy-start.1
  205.6 11.5 %fusion.12 = (bf16[128,1792]{1,0:T(8,128)(2,1)}, bf16[128,1792]{1,0:T(8,128)(2,1)}) fusion(bf16[128,1792]{1,0:T(8,128)(2,1)S(1)} %copy-done.4, bf16[128,1792]{1,0:T(8,128)(2,1)S(1)} %copy-done.5, bf16[128,4096]{1,0:T(8,128)(2,1)} %all-gather.5.cloned.1.call-done, bf16[1792,4096]{1,0:T(8,128)(2,1)} %param.21), kind=kOutput, calls=%fused_computation.23 | convolution fusion | flops 1882488832 | bytes 17563648 | tf_op jit(solution)/shard_map/dot_general | solution.py:80
  217.1 0.0 copy-done.1
  (12 shorter events, 0.1 us)
Async XLA Ops:
  7.2 3.0 %copy-start = (f32[1024]{0:T(1024)S(1)}, f32[1024]{0:T(1024)}, u32[]{:S(2)}) copy-start(f32[1024]{0:T(1024)} %param.14) | copy-start | bytes 12292
  7.2 33.2 %all-gather.3.cloned.1.call-start = ((), (), s32[]{:S(2)}) async-start(), calls=%async_computation.1 | async-start | bytes 2359296 | tf_op jit(solution)/shard_map/all_gather | solution.py:44
  7.9 95.0 %all-reduce.2.cloned.1.call-start = ((), (), s32[]{:S(2)}) async-start(), calls=%async_computation.2 | async-start | bytes 2097152 | tf_op jit(solution)/shard_map/psum | solution.py:61
  44.8 6.3 %copy-start.3 = (s32[1024]{0:T(1024)S(1)}, s32[1024]{0:T(1024)}, u32[]{:S(2)}) copy-start(s32[1024]{0:T(1024)} %param.15) | copy-start | bytes 12292
  50.8 124.7 %reduce-scatter.2.cloned.1.call-start = ((), (), s32[]{:S(2)}) async-start(), calls=%async_computation.3 | async-start | bytes 4718592 | tf_op jit(solution)/shard_map/reduce_scatter | solution.py:77
  51.1 9.5 %copy-start.2 = (f32[1024]{0:T(1024)S(1)}, f32[1024]{0:T(1024)}, u32[]{:S(2)}) copy-start(f32[1024]{0:T(1024)} %param.16) | copy-start | bytes 12292
  125.0 80.6 %copy-start.4 = (bf16[128,1792]{1,0:T(8,128)(2,1)S(1)}, bf16[128,1792]{1,0:T(8,128)(2,1)}, u32[]{:S(2)}) copy-start(bf16[128,1792]{1,0:T(8,128)(2,1)} %param.19) | copy-start | bytes 1376260
  125.0 80.6 %copy-start.5 = (bf16[128,1792]{1,0:T(8,128)(2,1)S(1)}, bf16[128,1792]{1,0:T(8,128)(2,1)}, u32[]{:S(2)}) copy-start(bf16[128,1792]{1,0:T(8,128)(2,1)} %param.20) | copy-start | bytes 1376260
  125.0 80.6 %all-gather.5.cloned.1.call-start = ((), (), s32[]{:S(2)}) async-start(), calls=%async_computation.4 | async-start | bytes 1310720 | tf_op jit(solution)/shard_map/all_gather | solution.py:81
  205.6 11.5 %copy-start.1 = (f32[1024]{0:T(1024)S(1)}, f32[1024]{0:T(1024)}, u32[]{:S(2)}) copy-start(f32[1024]{0:T(1024)} %param.14) | copy-start | bytes 12292
Sparse Core Ops, SparseCore 0:
  9.9 30.4 all-gather.2
  50.9 51.8 all-reduce.1
  125.1 50.4 reduce-scatter.1
  177.6 27.9 all-gather.4
where the time goes:
time: 224 us
  waiting for transfers between devices  144 us (64%)
  local copies, waits for them, and re-layouts  32.6 us (15%)
  matrix products  25.8 us (12%)
  between operations  13.9 us (6%)
  other arithmetic  7.04 us (3%)
    reduce_scatter x1, waiting for transfers between devices, on_device(): lax.psum_scatter(softmax_part - factor[:, None] * target_rows, 'wide', sc...  50.3 us
    psum x1, waiting for transfers between devices, on_device(): logits = lax.psum(partial_value, 'narrow')  42.2 us
    all_gather x1, waiting for transfers between devices, on_device(): lax.all_gather(head_grad, 'narrow', axis=1, tiled=True)  28.2 us
    all_gather x1, waiting for transfers between devices, on_device(): gathered = lax.all_gather(hidden, 'wide', axis=0, tiled=True)  22.3 us
    dot_general x1, matrix products, on_device(): lax.dot_general(lax.all_gather(head_grad, 'narrow', axis=1, tiled=True),...  11.5 us
    gather x1, local copies, waits for them, and re-layouts, on_device(): jnp.take(head_weight, jnp.clip(local_ids, 0, vocab_here - 1), axis=0)  9.44 us
    gather x1, local copies, waits for them, and re-layouts, on_device(): picked = jnp.take(weight_tiles, slot_tiles, axis=0)  6.13 us
    dot_general x1, matrix products, on_device(): jnp.einsum('srd,scd->src', row_blocks, picked, preferred_element_type=jnp...  6 us
  transfers between devices with their start and end apart: 4, of which 4 were waited for; matrix products, arithmetic and copies ran while one was open for 9% of the time, Pallas kernels for 0%

commit v1 on v0

--- a/solution.py
+++ b/solution.py
@@ -2,6 +2,7 @@
 import jax.numpy as jnp
 from jax import lax
 from jax.sharding import PartitionSpec as P
+from jax.lax import axis_size, ppermute
 
 TILE = 128
 
@@ -58,7 +59,13 @@
     )
     slot_lse = jnp.take(lse_blocks, slot_blocks, axis=0)
     slot_scale = jnp.take(scale_blocks, slot_blocks, axis=0)
-    logits = lax.psum(partial_value, "narrow")
+    n_dev_all = axis_size("narrow")
+    logits = partial_value
+    for dev_i in [
+        [(jj, jj ^ num) for jj in range(n_dev_all)] for num in (1, 2, 4, 8, 16) if num < n_dev_all
+    ]:
+        tall = ppermute(logits, "narrow", dev_i)
+        logits = logits + tall
     cell_probs = cell_weights(logits, slot_lse, slot_scale, slot_live)
     contrib = jnp.einsum("src,scd->srd", cell_probs, picked, preferred_element_type=jnp.float32)
     contrib = contrib.reshape(slot_count, TILE * features)

time: 224 us -> 245 us (1.094)
  waiting for transfers between devices: 144 us -> 163 us
  starting transfers between devices: 0.56 us -> 4.36 us
    ppermute x0 -> x2, waiting for transfers between devices: none -> 58.4 us  [on_device(): tall = ppermute(logits, 'narrow', dev_i)]
    psum x1 -> x0, waiting for transfers between devices: 42.2 us -> none  [on_device(): logits = lax.psum(partial_value, 'narrow')]
    ppermute x0 -> x2, starting transfers between devices: none -> 4.02 us  [on_device(): tall = ppermute(logits, 'narrow', dev_i)]
  transfers between devices with their start and end apart: 4 -> 5, of which waited for: 4 -> 5; matrix products, arithmetic and copies ran while one was open for 9% -> 8% of each run, Pallas kernels for 0% -> 0%
where the time goes in v1:
time: 245 us
  waiting for transfers between devices  163 us (67%)
  local copies, waits for them, and re-layouts  32.1 us (13%)
  matrix products  24.8 us (10%)
  between operations  13.9 us (6%)
  other arithmetic  7.15 us (3%)
  starting transfers between devices  4.36 us (2%)
    ppermute x2, waiting for transfers between devices, on_device(): tall = ppermute(logits, 'narrow', dev_i)  58.4 us
    reduce_scatter x1, waiting for transfers between devices, on_device(): lax.psum_scatter(softmax_part - factor[:, None] * target_rows, 'wide', sc...  51 us
    all_gather x1, waiting for transfers between devices, on_device(): lax.all_gather(head_grad, 'narrow', axis=1, tiled=True)  28.3 us
    all_gather x1, waiting for transfers between devices, on_device(): gathered = lax.all_gather(hidden, 'wide', axis=0, tiled=True)  24.1 us
    dot_general x1, matrix products, on_device(): lax.dot_general(lax.all_gather(head_grad, 'narrow', axis=1, tiled=True),...  11.5 us
    gather x1, local copies, waits for them, and re-layouts, on_device(): jnp.take(head_weight, jnp.clip(local_ids, 0, vocab_here - 1), axis=0)  9.62 us
    gather x1, local copies, waits for them, and re-layouts, on_device(): picked = jnp.take(weight_tiles, slot_tiles, axis=0)  6.14 us
    unnamed x14, local copies, waits for them, and re-layouts  5.65 us
  transfers between devices with their start and end apart: 5, of which 5 were waited for; matrix products, arithmetic and copies ran while one was open for 8% of the time, Pallas kernels for 0%

profile of v1, /device:TPU:0, one launch (start us, length us, event | category | flops | bytes accessed | tf_op | source)
XLA Modules:
  0.0 244.9 jit_solution(18208855697398647666)
XLA Ops:
  7.2 0.0 copy-start
  7.2 0.0 all-gather.3.cloned.1.call-start
  7.2 0.7 all-gather.3.cloned.1.call-update
  7.9 0.0 reduce-scatter.2.cloned.1.call-start
  8.0 0.7 iota_compare_fusion.2
  8.7 0.1 reshape.201
  8.8 0.1 lt.82
  8.9 0.1 mul.57
  8.9 0.8 copy.18
  9.7 0.1 mul.60
  9.8 0.1 reduce-window.8
  9.8 0.1 add_reduce_fusion
  9.9 0.2 convert_reduce_fusion
  10.1 6.1 %gather_fusion.1 = bf16[16,128,1024]{2,1,0:T(8,128)(2,1)} fusion(bf16[32,128,1024]{2,1,0:T(8,128)(2,1)} %bitcast.21, s32[1024]{0:T(1024)S(1)} %pad_clamp_fusion.1), kind=kCustom, calls=%fused_computation.3 | custom fusion | bytes 8388672 | tf_op jit(solution)/shard_map/jit(_take)/gather | solution.py:55
  16.3 24.1 %all-gather.3.cloned.1.call-done = bf16[1024,1024]{1,0:T(8,128)(2,1)} async-done(((bf16[128,1024]{1,0:T(8,128)(2,1)}), bf16[1024,1024]{1,0:T(8,128)(2,1)}) %all-gather.3.cloned.1.call-update) | async-done | bytes 2097168 | tf_op jit(solution)/shard_map/all_gather | solution.py:45
  40.4 4.4 %gather_fusion = bf16[16,128,1024]{2,1,0:T(8,128)(2,1)} fusion(bf16[8,128,1024]{2,1,0:T(8,128)(2,1)} %bitcast.24, s32[1024]{0:T(1024)S(1)} %pad_clamp_fusion.2), kind=kCustom, calls=%fused_computation.2 | custom fusion | bytes 8388672 | tf_op jit(solution)/shard_map/jit(_take)/gather | solution.py:56
  44.8 0.0 copy-start.2
  44.8 0.0 copy-start.3
  44.8 5.0 %fusion = f32[16,128,128]{2,1,0:T(8,128)S(1)} fusion(bf16[16,128,1024]{2,1,0:T(8,128)(2,1)} %gather_fusion, pred[16]{0:T(512)(128)(4,1)S(1)} %get-tuple-element.14, bf16[16,128,1024]{2,1,0:T(8,128)(2,1)} %gather_fusion.1, pred[16]{0:T(512)(128)(4,1)S(1)} %get-tuple-element.13), kind=kOutput, calls=%fused_computation.6 | convolution fusion | flops 541065216 | bytes 9437216 | tf_op jit(solution)/shard_map/srd,scd->src/dot_general | solution.py:57
  49.7 1.6 collective-permute-start
  51.3 0.0 copy-done
  51.3 0.6 gather_fusion.3
  51.9 0.0 copy-done.2
  51.9 0.6 gather_fusion.4
  52.5 22.6 %collective-permute-done = f32[16,128,128]{2,1,0:T(8,128)S(1)} collective-permute-done((f32[16,128,128]{2,1,0:T(8,128)S(1)}, f32[16,128,128]{2,1,0:T(8,128)S(1)}, u32[]{:S(2)}, u32[]{:S(2)}) %collective-permute-start) | collective-permute-done | bytes 1048608 | tf_op jit(solution)/shard_map/ppermute | solution.py:67
  75.1 0.1 add.63
  75.2 2.5 %collective-permute-start.1 = (f32[16,128,128]{2,1,0:T(8,128)S(1)}, f32[16,128,128]{2,1,0:T(8,128)}, u32[]{:S(2)}, u32[]{:S(2)}) collective-permute-start(f32[16,128,128]{2,1,0:T(8,128)S(1)} %add.63), channel_id=1, source_target_pairs={{0,2},{1,3},{2,0},{3,1},{4,6},{5,7},{6,4},{7,5},{8,10},{9,11},{10,... | collective-permute-start | bytes 3145736 | tf_op jit(solution)/shard_map/ppermute | solution.py:67
  77.7 0.0 copy-done.3
  77.7 9.6 %gather_fusion.2 = bf16[1024,1024]{1,0:T(8,128)(2,1)S(1)} fusion(bf16[4096,1024]{1,0:T(8,128)(2,1)} %param.13, s32[1024]{0:T(1024)S(1)} %fusion.21), kind=kCustom, calls=%fused_computation.4 | custom fusion | bytes 4198400 | tf_op jit(solution)/shard_map/jit(_take)/gather | solution.py:80
  87.4 0.1 broadcast_select_fusion.4
  87.5 35.8 %collective-permute-done.1 = f32[16,128,128]{2,1,0:T(8,128)} collective-permute-done((f32[16,128,128]{2,1,0:T(8,128)S(1)}, f32[16,128,128]{2,1,0:T(8,128)}, u32[]{:S(2)}, u32[]{:S(2)}) %collective-permute-start.1) | collective-permute-done | bytes 1048608 | tf_op jit(solution)/shard_map/ppermute | solution.py:67
  123.2 3.9 %fusion.4 = f32[16,128,1024]{2,1,0:T(8,128)S(1)} fusion(bf16[16,128,1024]{2,1,0:T(8,128)(2,1)} %gather_fusion.1, pred[16]{0:T(512)(128)(4,1)S(1)} %get-tuple-element.13, f32[16,128,128]{2,1,0:T(8,128)S(1)} %add.63, f32[16,128,128]{2,1,0:T(8,128)} %collective-permute-done.1, f32[16,128]{1,0:T(8,128)S(1)} %get-tuple-element.10, ...), kind=kOutput, calls=%fused_computation.11 | convolution fusion | flops 540278784 | bytes 14696480 | tf_op jit(solution)/shard_map/src,scd->srd/dot_general | solution.py:70
  127.1 4.9 %copy.19 = f32[2,8,128,1024]{3,1,2,0:T(8,128)S(1)} copy(f32[2,8,128,1024]{3,2,1,0:T(8,128)S(1)} %bitcast.22) | data formatting | bytes 16777216
  132.0 4.4 %fusion.19 = f32[8,131072]{1,0:T(8,128)} fusion(f32[16,131072]{1,0:T(8,128)S(1)} %bitcast.23, s32[16]{0:T(128)S(1)} %get-tuple-element.6, pred[16]{0:T(512)(128)(4,1)S(1)} %broadcast_compare_fusion), kind=kOutput, calls=%fused_computation.43 | convolution fusion | flops 201326848 | bytes 12582992 | tf_op jit(solution)/shard_map/dot_general | solution.py:75
  136.4 4.9 %reshape.152 = f32[1024,1024]{1,0:T(8,128)} reshape(f32[8,131072]{1,0:T(8,128)} %fusion.19) | data formatting | bytes 8388608 | tf_op jit(solution)/shard_map/reshape | solution.py:77
  141.3 4.0 %multiply_subtract_fusion = f32[1024,1024]{1,0:T(8,128)} fusion(f32[1024,1024]{1,0:T(8,128)} %reshape.152, bf16[1024,1024]{1,0:T(8,128)(2,1)S(1)} %gather_fusion.2, f32[1024]{0:T(1024)S(1)} %and_select_fusion, pred[1024]{0:T(1024)(128)(4,1)S(1)} %compare_and_fusion), kind=kLoop, calls=%fused_computation.5 | loop fusion | flops 4194304 | bytes 10490880 | tf_op jit(solution)/shard_map/sub | solution.py:85
  145.3 0.0 copy-start.4
  145.3 0.0 copy-start.5
  145.3 0.0 reduce-scatter.2.cloned.1.call-update
  145.4 0.3 all-gather.5.cloned.1.call-start
  145.6 51.0 %reduce-scatter.2.cloned.1.call-done = f32[128,1024]{1,0:T(8,128)} async-done(((f32[1024,1024]{1,0:T(8,128)}), f32[128,1024]{1,0:T(8,128)}) %reduce-scatter.2.cloned.1.call-update) | async-done | bytes 524304 | tf_op jit(solution)/shard_map/reduce_scatter | solution.py:84
  196.7 1.8 convert_element_type.45
  198.4 0.0 all-gather.5.cloned.1.call-update
  198.5 28.3 %all-gather.5.cloned.1.call-done = bf16[128,4096]{1,0:T(8,128)(2,1)} async-done(((bf16[128,1024]{1,0:T(8,128)(2,1)}), bf16[128,4096]{1,0:T(8,128)(2,1)}) %all-gather.5.cloned.1.call-update) | async-done | bytes 1048592 | tf_op jit(solution)/shard_map/all_gather | solution.py:88
  226.8 0.0 copy-done.4
  226.8 0.0 copy-done.5
  226.8 0.0 copy-start.1
  226.8 11.5 %fusion.12 = (bf16[128,1792]{1,0:T(8,128)(2,1)}, bf16[128,1792]{1,0:T(8,128)(2,1)}) fusion(bf16[128,1792]{1,0:T(8,128)(2,1)S(1)} %copy-done.4, bf16[128,1792]{1,0:T(8,128)(2,1)S(1)} %copy-done.5, bf16[128,4096]{1,0:T(8,128)(2,1)} %all-gather.5.cloned.1.call-done, bf16[1792,4096]{1,0:T(8,128)(2,1)} %param.21), kind=kOutput, calls=%fused_computation.23 | convolution fusion | flops 1882488832 | bytes 17563648 | tf_op jit(solution)/shard_map/dot_general | solution.py:87
  238.3 0.0 copy-done.1
  (12 shorter events, 0.1 us)
Async XLA Ops:
  7.2 44.2 %copy-start = (f32[1024]{0:T(1024)S(1)}, f32[1024]{0:T(1024)}, u32[]{:S(2)}) copy-start(f32[1024]{0:T(1024)} %param.14) | copy-start | bytes 12292
  7.2 33.2 %all-gather.3.cloned.1.call-start = ((), (), s32[]{:S(2)}) async-start(), calls=%async_computation.1 | async-start | bytes 2359296 | tf_op jit(solution)/shard_map/all_gather | solution.py:45
  7.9 188.7 %reduce-scatter.2.cloned.1.call-start = ((), (), s32[]{:S(2)}) async-start(), calls=%async_computation.2 | async-start | bytes 4718592 | tf_op jit(solution)/shard_map/reduce_scatter | solution.py:84
  44.8 7.1 %copy-start.2 = (f32[1024]{0:T(1024)S(1)}, f32[1024]{0:T(1024)}, u32[]{:S(2)}) copy-start(f32[1024]{0:T(1024)} %param.16) | copy-start | bytes 12292
  44.8 32.9 %copy-start.3 = (s32[1024]{0:T(1024)S(1)}, s32[1024]{0:T(1024)}, u32[]{:S(2)}) copy-start(s32[1024]{0:T(1024)} %param.15) | copy-start | bytes 12292
  49.7 25.4 %collective-permute-start = (f32[16,128,128]{2,1,0:T(8,128)S(1)}, f32[16,128,128]{2,1,0:T(8,128)S(1)}, u32[]{:S(2)}, u32[]{:S(2)}) collective-permute-start(f32[16,128,128]{2,1,0:T(8,128)S(1)} %fusion), channel_id=1, source_target_pairs={{0,1},{1,0},{2,3},{3,2},{4,5},{5,4},{6,7},{7,6},{8,9},{9,8},{10,11... | collective-permute-start | bytes 3145736 | tf_op jit(solution)/shard_map/ppermute | solution.py:67
  75.2 48.0 %collective-permute-start.1 = (f32[16,128,128]{2,1,0:T(8,128)S(1)}, f32[16,128,128]{2,1,0:T(8,128)}, u32[]{:S(2)}, u32[]{:S(2)}) collective-permute-start(f32[16,128,128]{2,1,0:T(8,128)S(1)} %add.63), channel_id=1, source_target_pairs={{0,2},{1,3},{2,0},{3,1},{4,6},{5,7},{6,4},{7,5},{8,10},{9,11},{10,... | collective-permute-start | bytes 3145736 | tf_op jit(solution)/shard_map/ppermute | solution.py:67
  145.3 81.5 %copy-start.4 = (bf16[128,1792]{1,0:T(8,128)(2,1)S(1)}, bf16[128,1792]{1,0:T(8,128)(2,1)}, u32[]{:S(2)}) copy-start(bf16[128,1792]{1,0:T(8,128)(2,1)} %param.19) | copy-start | bytes 1376260
  145.3 81.5 %copy-start.5 = (bf16[128,1792]{1,0:T(8,128)(2,1)S(1)}, bf16[128,1792]{1,0:T(8,128)(2,1)}, u32[]{:S(2)}) copy-start(bf16[128,1792]{1,0:T(8,128)(2,1)} %param.20) | copy-start | bytes 1376260
  145.4 81.4 %all-gather.5.cloned.1.call-start = ((), (), s32[]{:S(2)}) async-start(), calls=%async_computation.3 | async-start | bytes 1310720 | tf_op jit(solution)/shard_map/all_gather | solution.py:88
  226.8 11.5 %copy-start.1 = (f32[1024]{0:T(1024)S(1)}, f32[1024]{0:T(1024)}, u32[]{:S(2)}) copy-start(f32[1024]{0:T(1024)} %param.14) | copy-start | bytes 12292
Sparse Core Ops, SparseCore 0:
  9.9 30.4 all-gather.2
  145.5 51.1 reduce-scatter.1
  198.8 27.9 all-gather.4
